TPU v7x, 32 devices: a whole 2x2x4 slice. The times are simulated.
32 devices in a mesh: seq: 2 (over core), ctx: 4 (over y, x), fsdp: 4 (over z).
Axes of the slice: x: 2, y: 2, z: 4, core: 2. Of those that a mesh axis runs over, the one named last changes fastest.
Arguments:
- tokens: bfloat16 [2, 2048, 768], P('seq', ('ctx', 'fsdp')), may hold values from -6 to 6
- documents: int32 [2, 2048], P('seq', ('ctx', 'fsdp')), may hold values from 0 to 1, as said below
- joint_weight: bfloat16 [768, 2304], P(('seq', 'fsdp')), may hold values from -0.21875 to 0.21875
- query_bias: bfloat16 [768], P(('seq', 'fsdp')), may hold values from -0.59765625 to 0.59765625
- value_bias: bfloat16 [768], P(('seq', 'fsdp')), may hold values from -0.119628906 to 0.119628906
- mixer_weight: bfloat16 [768, 768], P(('seq', 'fsdp')), may hold values from -4 to 4
- mixer_bias: bfloat16 [768], P(('seq', 'fsdp')), may hold values from -0.59765625 to 0.59765625
- first_gain: bfloat16 [768], P(('seq', 'fsdp')), may hold values from 0.5 to 1.5
- first_bias: bfloat16 [768], P(('seq', 'fsdp')), may hold values from -0.59765625 to 0.59765625
- hidden_weight: bfloat16 [768, 3072], P(('seq', 'fsdp')), may hold values from -0.21875 to 0.21875
- hidden_bias: bfloat16 [3072], P(('seq', 'fsdp')), may hold values from -0.59765625 to 0.59765625
- return_weight: bfloat16 [3072, 768], P(('seq', 'fsdp')), may hold values from -0.109375 to 0.109375
- return_bias: bfloat16 [768], P(('seq', 'fsdp')), may hold values from -0.59765625 to 0.59765625
- second_gain: bfloat16 [768], P(('seq', 'fsdp')), may hold values from 0.5 to 1.5
- second_bias: bfloat16 [768], P(('seq', 'fsdp')), may hold values from -0.59765625 to 0.59765625
- cotangent: bfloat16 [2, 2048, 768], P('seq', ('ctx', 'fsdp')), may hold values from -6 to 6
Outputs:
- result: bfloat16 [2, 2048, 768], P('seq', ('ctx', 'fsdp'))
- tokens_grad: float32 [2, 2048, 768], P('seq', ('ctx', 'fsdp'))
- joint_grad: float32 [768, 2304], P(('seq', 'fsdp'))
- query_grad: float32 [768], P(('seq', 'fsdp'))
- value_grad: float32 [768], P(('seq', 'fsdp'))
- mixer_grad: float32 [768, 768], P(('seq', 'fsdp'))
- mixer_drift: float32 [768], P(('seq', 'fsdp'))
- first_scale: float32 [768], P(('seq', 'fsdp'))
- first_drift: float32 [768], P(('seq', 'fsdp'))
- hidden_grad: float32 [768, 3072], P(('seq', 'fsdp'))
- hidden_drift: float32 [3072], P(('seq', 'fsdp'))
- return_grad: float32 [3072, 768], P(('seq', 'fsdp'))
- return_drift: float32 [768], P(('seq', 'fsdp'))
- second_scale: float32 [768], P(('seq', 'fsdp'))
- second_drift: float32 [768], P(('seq', 'fsdp'))
Inputs may be any that keep to these rules, and one draw needn't show every extreme that they name: Along each sequence the document numbers start at 0 on the first token and rise by one at each new document; every sequence holds 2 documents. Each sequence holds one document of exactly 1536 tokens that starts at a multiple of 512; every other document has at most 896 tokens.
All inputs are finite; a program needn't handle non-finite values.
Results may differ from a plain program's by a relative error of at most 0.02.
Values may be sent and summed in bfloat16 or wider, within the bound.
A program may use at most 256 MiB of HBM per device.

v0:
```python
import math

import jax
import jax.numpy as jnp
from jax import lax
from jax.sharding import PartitionSpec as P

HEADS = 12
HEAD_DIM = 64


def contract_rows(operand, other):
    return lax.dot_general(
        operand, other, (((0,), (0,)), ((), ())), preferred_element_type=jnp.float32
    )


def contract_cols(operand, other):
    return lax.dot_general(
        operand, other, (((1,), (1,)), ((), ())), preferred_element_type=jnp.float32
    )


def norm_forward(values, gain, shift):
    center = values - jnp.mean(values, axis=-1, keepdims=True)
    inverse = lax.rsqrt(jnp.mean(center * center, axis=-1, keepdims=True) + 1e-06)
    normed = center * inverse
    return (normed * gain + shift, normed, inverse)


def norm_backward(upstream, normed, inverse, gain):
    gain_grad = jnp.sum(upstream * normed, axis=0)
    shift_grad = jnp.sum(upstream, axis=0)
    scaled = upstream * gain
    plain_mean = jnp.mean(scaled, axis=-1, keepdims=True)
    cross_mean = jnp.mean(scaled * normed, axis=-1, keepdims=True)
    return (inverse * (scaled - plain_mean - normed * cross_mean), gain_grad, shift_grad)


def gelu_exact(values):
    return jax.nn.gelu(values, approximate=False)


def by_blocks(step_fn, running, incoming, tok_rows):
    row_count = incoming[0].shape[0]
    shard_count = row_count // tok_rows
    limit_shards = max(1, 1024 // tok_rows)
    group_size = math.gcd(shard_count, 1 << limit_shards.bit_length() - 1)
    block_rows = group_size * tok_rows
    turn_count = row_count // block_rows
    stacked = tuple(
        (member.reshape((turn_count, block_rows) + member.shape[1:]) for member in incoming)
    )

    def scan_step(current, element):
        portion, number = element
        return (step_fn(current, portion, number * block_rows), None)

    running, unused = lax.scan(
        scan_step, running, (stacked, jnp.arange(turn_count, dtype=jnp.int32))
    )
    return running


def shards(
    tokens,
    documents,
    joint_weight,
    query_bias,
    value_bias,
    mixer_weight,
    mixer_bias,
    first_gain,
    first_bias,
    hidden_weight,
    hidden_bias,
    return_weight,
    return_bias,
    second_gain,
    second_bias,
    cotangent,
):
    inputs = tokens[0]
    tok_rows = inputs.shape[0]
    model_width = inputs.shape[1]
    factor = float(HEAD_DIM) ** (-0.5)
    joint_full, mixer_full, query_full, value_full, offset_full, gain_first, bias_first = (
        lax.all_gather(joint_weight, ("seq", "fsdp"), axis=0, tiled=True),
        lax.all_gather(mixer_weight, ("seq", "fsdp"), axis=0, tiled=True),
        lax.all_gather(query_bias, ("seq", "fsdp"), axis=0, tiled=True),
        lax.all_gather(value_bias, ("seq", "fsdp"), axis=0, tiled=True),
        lax.all_gather(mixer_bias, ("seq", "fsdp"), axis=0, tiled=True),
        lax.all_gather(first_gain, ("seq", "fsdp"), axis=0, tiled=True),
        lax.all_gather(first_bias, ("seq", "fsdp"), axis=0, tiled=True),
    )
    projected = jnp.dot(inputs, joint_full, preferred_element_type=jnp.float32)
    queries = (projected[:, :model_width] + query_full.astype(jnp.float32)).astype(jnp.bfloat16)
    keys_loc = projected[:, model_width : 2 * model_width].astype(jnp.bfloat16)
    values_loc = (projected[:, 2 * model_width :] + value_full.astype(jnp.float32)).astype(
        jnp.bfloat16
    )
    doc_rows = documents[0].astype(jnp.float32) + 1.0
    doc_send = doc_rows.astype(jnp.bfloat16)
    query_heads = queries.reshape(tok_rows, HEADS, HEAD_DIM)
    key_heads = keys_loc.reshape(tok_rows, HEADS, HEAD_DIM)
    value_heads = values_loc.reshape(tok_rows, HEADS, HEAD_DIM)

    def forward_step(running, incoming, offset):
        peak_old, total_old, weighted_old = running
        key_piece, value_piece, doc_piece = incoming
        row_count = key_piece.shape[0]
        key_split = key_piece.reshape(row_count, HEADS, HEAD_DIM)
        value_split = value_piece.reshape(row_count, HEADS, HEAD_DIM)
        scores = (
            jnp.einsum("qhd,khd->hqk", query_heads, key_split, preferred_element_type=jnp.float32)
            * factor
        )
        allowed = (doc_rows[:, None] == doc_piece.astype(jnp.float32)[None, :])[None]
        masked = jnp.where(allowed, scores, -1e30)
        peak_new = jnp.maximum(peak_old, jnp.max(masked, axis=-1))
        weights = jnp.where(allowed, jnp.exp(masked - peak_new[:, :, None]), 0.0)
        rescale = jnp.exp(peak_old - peak_new)
        total_new = total_old * rescale + jnp.sum(weights, axis=-1)
        blended = jnp.einsum(
            "hqk,khd->qhd",
            weights.astype(jnp.bfloat16),
            value_split,
            preferred_element_type=jnp.float32,
        )
        weighted_new = (
            weighted_old.reshape(tok_rows, HEADS, HEAD_DIM) * jnp.transpose(rescale)[:, :, None]
            + blended
        )
        return (peak_new, total_new, weighted_new.reshape(tok_rows, model_width))

    start_fwd = (
        jnp.full((HEADS, tok_rows), -1e30, jnp.float32),
        jnp.zeros((HEADS, tok_rows), jnp.float32),
        jnp.zeros((tok_rows, model_width), jnp.float32),
    )
    row_peak, row_total, weighted = by_blocks(
        forward_step,
        start_fwd,
        (
            lax.all_gather(keys_loc, ("ctx", "fsdp"), axis=0, tiled=True),
            lax.all_gather(values_loc, ("ctx", "fsdp"), axis=0, tiled=True),
            lax.all_gather(doc_send, ("ctx", "fsdp"), axis=0, tiled=True),
        ),
        tok_rows,
    )
    attention = (
        weighted.reshape(tok_rows, HEADS, HEAD_DIM) / jnp.transpose(row_total)[:, :, None]
    ).reshape(tok_rows, model_width)
    mixed_low = attention.astype(jnp.bfloat16)
    log_total = row_peak + jnp.log(row_total)
    branch = jnp.dot(
        mixed_low, mixer_full, preferred_element_type=jnp.float32
    ) + offset_full.astype(jnp.float32)
    first_norm, first_hat, first_inv = norm_forward(
        inputs.astype(jnp.float32) + branch,
        gain_first.astype(jnp.float32),
        bias_first.astype(jnp.float32),
    )
    hidden_full, return_full, inner_shift, outer_shift, gain_second, bias_second = (
        lax.all_gather(hidden_weight, ("seq", "fsdp"), axis=0, tiled=True),
        lax.all_gather(return_weight, ("seq", "fsdp"), axis=0, tiled=True),
        lax.all_gather(hidden_bias, ("seq", "fsdp"), axis=0, tiled=True),
        lax.all_gather(return_bias, ("seq", "fsdp"), axis=0, tiled=True),
        lax.all_gather(second_gain, ("seq", "fsdp"), axis=0, tiled=True),
        lax.all_gather(second_bias, ("seq", "fsdp"), axis=0, tiled=True),
    )
    first_low = first_norm.astype(jnp.bfloat16)
    inner = jnp.dot(
        first_low, hidden_full, preferred_element_type=jnp.float32
    ) + inner_shift.astype(jnp.float32)
    acted, gelu_pull = jax.vjp(gelu_exact, inner)
    acted_low = acted.astype(jnp.bfloat16)
    second_in = (
        first_norm
        + jnp.dot(acted_low, return_full, preferred_element_type=jnp.float32)
        + outer_shift.astype(jnp.float32)
    )
    outcome, second_hat, second_inv = norm_forward(
        second_in, gain_second.astype(jnp.float32), bias_second.astype(jnp.float32)
    )
    upstream = cotangent[0].astype(jnp.float32)
    back_second, second_scale, second_drift = norm_backward(
        upstream, second_hat, second_inv, gain_second.astype(jnp.float32)
    )
    back_return = back_second.astype(jnp.bfloat16)
    return_drift = jnp.sum(back_return.astype(jnp.float32), axis=0)
    return_grad = contract_rows(acted_low, back_return)
    back_inner = gelu_pull(contract_cols(back_return, return_full))[0].astype(jnp.bfloat16)
    hidden_drift = jnp.sum(back_inner.astype(jnp.float32), axis=0)
    hidden_grad = contract_rows(first_low, back_inner)
    back_first = back_second + contract_cols(back_inner, hidden_full)
    back_first_in, first_scale, first_drift = norm_backward(
        back_first, first_hat, first_inv, gain_first.astype(jnp.float32)
    )
    back_mix = back_first_in.astype(jnp.bfloat16)
    mixer_drift = jnp.sum(back_mix.astype(jnp.float32), axis=0)
    mixer_grad = contract_rows(mixed_low, back_mix)
    back_att = contract_cols(back_mix, mixer_full).astype(jnp.bfloat16)
    delta = jnp.transpose(
        jnp.sum(
            (back_att.astype(jnp.float32) * attention).reshape(tok_rows, HEADS, HEAD_DIM), axis=-1
        )
    )
    stats_lse, stats_delta = (
        lax.all_gather(log_total, ("ctx", "fsdp"), axis=1, tiled=True),
        lax.all_gather(delta, ("ctx", "fsdp"), axis=1, tiled=True),
    )
    back_heads = back_att.reshape(tok_rows, HEADS, HEAD_DIM)

    def backward_step(running, incoming, offset):
        query_back, key_back, value_back = running
        query_piece, key_piece, value_piece, grad_piece, doc_piece = incoming
        row_count = key_piece.shape[0]
        query_split = query_piece.reshape(row_count, HEADS, HEAD_DIM)
        key_split = key_piece.reshape(row_count, HEADS, HEAD_DIM)
        value_split = value_piece.reshape(row_count, HEADS, HEAD_DIM)
        grad_split = grad_piece.reshape(row_count, HEADS, HEAD_DIM)
        lse_piece = lax.dynamic_slice_in_dim(stats_lse, offset, row_count, 1)
        delta_piece = lax.dynamic_slice_in_dim(stats_delta, offset, row_count, 1)
        allowed = doc_rows[:, None] == doc_piece.astype(jnp.float32)[None, :]
        scores = (
            jnp.einsum("qhd,khd->hqk", query_heads, key_split, preferred_element_type=jnp.float32)
            * factor
        )
        probs = jnp.where(allowed[None], jnp.exp(scores - log_total[:, :, None]), 0.0)
        dprobs = jnp.einsum(
            "qhd,khd->hqk", back_heads, value_split, preferred_element_type=jnp.float32
        )
        dscores = (probs * (dprobs - delta[:, :, None])).astype(jnp.bfloat16)
        query_back = query_back + factor * jnp.einsum(
            "hqk,khd->qhd", dscores, key_split, preferred_element_type=jnp.float32
        ).reshape(tok_rows, model_width)
        scores_rev = (
            jnp.einsum("qhd,khd->hqk", query_split, key_heads, preferred_element_type=jnp.float32)
            * factor
        )
        probs_rev = jnp.where(
            jnp.transpose(allowed)[None], jnp.exp(scores_rev - lse_piece[:, :, None]), 0.0
        )
        value_back = value_back + jnp.einsum(
            "hqk,qhd->khd",
            probs_rev.astype(jnp.bfloat16),
            grad_split,
            preferred_element_type=jnp.float32,
        ).reshape(tok_rows, model_width)
        dprobs_rev = jnp.einsum(
            "qhd,khd->hqk", grad_split, value_heads, preferred_element_type=jnp.float32
        )
        dscores_rev = (probs_rev * (dprobs_rev - delta_piece[:, :, None])).astype(jnp.bfloat16)
        key_back = key_back + factor * jnp.einsum(
            "hqk,qhd->khd", dscores_rev, query_split, preferred_element_type=jnp.float32
        ).reshape(tok_rows, model_width)
        return (query_back, key_back, value_back)

    start_back = (
        jnp.zeros((tok_rows, model_width), jnp.float32),
        jnp.zeros((tok_rows, model_width), jnp.float32),
        jnp.zeros((tok_rows, model_width), jnp.float32),
    )
    query_back, key_back, value_back = by_blocks(
        backward_step,
        start_back,
        (
            lax.all_gather(queries, ("ctx", "fsdp"), axis=0, tiled=True),
            lax.all_gather(keys_loc, ("ctx", "fsdp"), axis=0, tiled=True),
            lax.all_gather(values_loc, ("ctx", "fsdp"), axis=0, tiled=True),
            lax.all_gather(back_att, ("ctx", "fsdp"), axis=0, tiled=True),
            lax.all_gather(doc_send, ("ctx", "fsdp"), axis=0, tiled=True),
        ),
        tok_rows,
    )
    proj_back = jnp.concatenate(
        [
            query_back.astype(jnp.bfloat16),
            key_back.astype(jnp.bfloat16),
            value_back.astype(jnp.bfloat16),
        ],
        axis=1,
    )
    joint_grad = contract_rows(inputs, proj_back)
    query_grad = jnp.sum(proj_back[:, :model_width].astype(jnp.float32), axis=0)
    value_grad = jnp.sum(proj_back[:, 2 * model_width :].astype(jnp.float32), axis=0)
    tokens_grad = back_first_in + contract_cols(proj_back, joint_full)
    joint_part, mixer_part, query_part, value_part, drift_part, scale_part, shift_part = (
        lax.psum_scatter(
            joint_grad.astype(jnp.bfloat16), ("seq", "fsdp"), scatter_dimension=0, tiled=True
        ).astype(jnp.float32),
        lax.psum_scatter(
            mixer_grad.astype(jnp.bfloat16), ("seq", "fsdp"), scatter_dimension=0, tiled=True
        ).astype(jnp.float32),
        lax.psum_scatter(
            query_grad.astype(jnp.bfloat16), ("seq", "fsdp"), scatter_dimension=0, tiled=True
        ).astype(jnp.float32),
        lax.psum_scatter(
            value_grad.astype(jnp.bfloat16), ("seq", "fsdp"), scatter_dimension=0, tiled=True
        ).astype(jnp.float32),
        lax.psum_scatter(
            mixer_drift.astype(jnp.bfloat16), ("seq", "fsdp"), scatter_dimension=0, tiled=True
        ).astype(jnp.float32),
        lax.psum_scatter(
            first_scale.astype(jnp.bfloat16), ("seq", "fsdp"), scatter_dimension=0, tiled=True
        ).astype(jnp.float32),
        lax.psum_scatter(
            first_drift.astype(jnp.bfloat16), ("seq", "fsdp"), scatter_dimension=0, tiled=True
        ).astype(jnp.float32),
    )
    joint_sum, mixer_sum, query_sum, value_sum, drift_sum, scale_sum, shift_sum = (
        lax.psum(joint_part.astype(jnp.bfloat16), "ctx").astype(jnp.float32),
        lax.psum(mixer_part.astype(jnp.bfloat16), "ctx").astype(jnp.float32),
        lax.psum(query_part.astype(jnp.bfloat16), "ctx").astype(jnp.float32),
        lax.psum(value_part.astype(jnp.bfloat16), "ctx").astype(jnp.float32),
        lax.psum(drift_part.astype(jnp.bfloat16), "ctx").astype(jnp.float32),
        lax.psum(scale_part.astype(jnp.bfloat16), "ctx").astype(jnp.float32),
        lax.psum(shift_part.astype(jnp.bfloat16), "ctx").astype(jnp.float32),
    )
    hidden_part, return_part, inner_part, outer_part, gain_part, bias_part = (
        lax.psum_scatter(
            hidden_grad.astype(jnp.bfloat16), ("seq", "fsdp"), scatter_dimension=0, tiled=True
        ).astype(jnp.float32),
        lax.psum_scatter(
            return_grad.astype(jnp.bfloat16), ("seq", "fsdp"), scatter_dimension=0, tiled=True
        ).astype(jnp.float32),
        lax.psum_scatter(
            hidden_drift.astype(jnp.bfloat16), ("seq", "fsdp"), scatter_dimension=0, tiled=True
        ).astype(jnp.float32),
        lax.psum_scatter(
            return_drift.astype(jnp.bfloat16), ("seq", "fsdp"), scatter_dimension=0, tiled=True
        ).astype(jnp.float32),
        lax.psum_scatter(
            second_scale.astype(jnp.bfloat16), ("seq", "fsdp"), scatter_dimension=0, tiled=True
        ).astype(jnp.float32),
        lax.psum_scatter(
            second_drift.astype(jnp.bfloat16), ("seq", "fsdp"), scatter_dimension=0, tiled=True
        ).astype(jnp.float32),
    )
    hidden_sum, return_sum, inner_sum, outer_sum, gain_sum, bias_sum = (
        lax.psum(hidden_part.astype(jnp.bfloat16), "ctx").astype(jnp.float32),
        lax.psum(return_part.astype(jnp.bfloat16), "ctx").astype(jnp.float32),
        lax.psum(inner_part.astype(jnp.bfloat16), "ctx").astype(jnp.float32),
        lax.psum(outer_part.astype(jnp.bfloat16), "ctx").astype(jnp.float32),
        lax.psum(gain_part.astype(jnp.bfloat16), "ctx").astype(jnp.float32),
        lax.psum(bias_part.astype(jnp.bfloat16), "ctx").astype(jnp.float32),
    )
    return (
        outcome[None].astype(jnp.bfloat16),
        tokens_grad[None],
        joint_sum,
        query_sum,
        value_sum,
        mixer_sum,
        drift_sum,
        scale_sum,
        shift_sum,
        hidden_sum,
        inner_sum,
        return_sum,
        outer_sum,
        gain_sum,
        bias_sum,
    )


def solution(mesh):
    return jax.shard_map(
        shards,
        mesh=mesh,
        in_specs=(
            P("seq", ("ctx", "fsdp"), None),
            P("seq", ("ctx", "fsdp")),
            P(("seq", "fsdp"), None),
            P(("seq", "fsdp")),
            P(("seq", "fsdp")),
            P(("seq", "fsdp"), None),
            P(("seq", "fsdp")),
            P(("seq", "fsdp")),
            P(("seq", "fsdp")),
            P(("seq", "fsdp"), None),
            P(("seq", "fsdp")),
            P(("seq", "fsdp"), None),
            P(("seq", "fsdp")),
            P(("seq", "fsdp")),
            P(("seq", "fsdp")),
            P("seq", ("ctx", "fsdp"), None),
        ),
        out_specs=(
            P("seq", ("ctx", "fsdp"), None),
            P("seq", ("ctx", "fsdp"), None),
            P(("seq", "fsdp"), None),
            P(("seq", "fsdp")),
            P(("seq", "fsdp")),
            P(("seq", "fsdp"), None),
            P(("seq", "fsdp")),
            P(("seq", "fsdp")),
            P(("seq", "fsdp")),
            P(("seq", "fsdp"), None),
            P(("seq", "fsdp")),
            P(("seq", "fsdp"), None),
            P(("seq", "fsdp")),
            P(("seq", "fsdp")),
            P(("seq", "fsdp")),
        ),
        check_vma=False,
    )
```

profile of v0, /device:TPU:0, one launch (start us, length us, event | category | flops | bytes accessed | tf_op | source)
XLA Modules:
  0.0 960.6 jit_solution(3067120699255219177)
XLA Ops:
  15.8 32.4 %all-reduce.18 = (bf16[768]{0:T(1024)(128)(2,1)S(1)}, bf16[768]{0:T(1024)(128)(2,1)S(1)}, bf16[768]{0:T(1024)(128)(2,1)S(1)}, bf16[768]{0:T(1024)(128)(2,1)S(1)}...) all-reduce(bf16[768]{0:T(1024)(128)(2,1)S(1)} %dynamic-update-slice, ...), channel_id=1, replica_groups=mesh['seq'=2,'ctx'=4,'fsdp'=4] {'seq','fsdp'}, use_global_device_ids=true, to_apply=%add | all-reduce | flops 5376 | bytes 21504
  48.2 6.8 all-gather.11.cloned.1.call-done
  61.7 38.5 %all-gather = bf16[16,1,128]{2,1,0:T(2,128)(2,1)S(1)} all-gather(bf16[1,1,128]{2,1,0:T(2,128)(2,1)S(1)} %get-tuple-element.505), channel_id=1, replica_groups=mesh['seq'=2,'ctx'=4,'fsdp'=4] {'ctx','fsdp'}, dimensions={0}, use_global_device_ids=true | all-gather | bytes 4352 | tf_op jit(solution)/shard_map/all_gather | solution.py:147
  100.2 21.8 %all-gather.1 = bf16[8,1,384]{2,1,0:T(2,128)(2,1)S(1)} all-gather(bf16[1,1,384]{2,1,0:T(2,128)(2,1)S(1)} %reshape.292), channel_id=1, replica_groups=mesh['seq'=2,'ctx'=4,'fsdp'=4] {'seq','fsdp'}, dimensions={0}, use_global_device_ids=true | all-gather | bytes 6912 | tf_op jit(solution)/shard_map/all_gather | solution.py:167
  130.4 65.3 %all-gather.13.cloned.1.call-done = bf16[2048,768]{1,0:T(8,128)(2,1)} async-done(((bf16[128,768]{1,0:T(8,128)(2,1)}), bf16[2048,768]{1,0:T(8,128)(2,1)}) %all-gather.13.cloned.1.call-update) | async-done | bytes 3145744 | tf_op jit(solution)/shard_map/all_gather | solution.py:145
  200.3 27.4 %while.30 = (s32[]{:T(128)}, f32[12,128]{1,0:T(8,128)S(1)}, f32[12,128]{1,0:T(8,128)S(1)}, f32[128,768]{0,1:T(8,128)S(1)}, f32[128]{0:T(128)}, /*index=5*/bf16[2...) while((s32[]{:T(128)}, f32[12,128]{1,0:T(8,128)S(1)}, ...), condition=%wide.region_3.4_spmd.clone, body=%wide.region_0.3_spmd.clone.sunk | while | flops 423438336 | bytes 55093912 | solution.py:59
  230.7 40.6 %all-gather.19.cloned.1.call-done = bf16[768,3072]{1,0:T(8,128)(2,1)} async-done(((bf16[96,3072]{1,0:T(8,128)(2,1)}), bf16[768,3072]{1,0:T(8,128)(2,1)}) %all-gather.19.cloned.1.call-update) | async-done | bytes 4718608 | tf_op jit(solution)/shard_map/all_gather | solution.py:165
  271.2 8.6 multiply_convert_fusion.4
  279.8 43.4 %all-gather.21.cloned.1.call-done = bf16[3072,768]{1,0:T(8,128)(2,1)} async-done(((bf16[384,768]{1,0:T(8,128)(2,1)}), bf16[3072,768]{1,0:T(8,128)(2,1)}) %all-gather.21.cloned.1.call-update) | async-done | bytes 4718608 | tf_op jit(solution)/shard_map/all_gather | solution.py:166
  340.4 43.1 %all_gather.82 = f32[12,2048]{1,0:T(8,128)} all-gather(f32[12,128]{1,0:T(8,128)} %bitcast.14), channel_id=1, replica_groups=mesh['seq'=2,'ctx'=4,'fsdp'=4] {'ctx','fsdp'}, dimensions={1}, use_global_device_ids=true | all-gather | bytes 104448 | tf_op jit(solution)/shard_map/all_gather | solution.py:211
  384.0 39.5 %all_gather.80 = f32[12,2048]{1,0:T(8,128)} all-gather(f32[12,128]{1,0:T(8,128)} %log_add_fusion), channel_id=1, replica_groups=mesh['seq'=2,'ctx'=4,'fsdp'=4] {'ctx','fsdp'}, dimensions={1}, use_global_device_ids=true | all-gather | bytes 104448 | tf_op jit(solution)/shard_map/all_gather | solution.py:210
  423.6 40.3 %all-gather.25.cloned.1.call-done = bf16[2048,768]{1,0:T(8,128)(2,1)} async-done(((bf16[128,768]{1,0:T(8,128)(2,1)}), bf16[2048,768]{1,0:T(8,128)(2,1)}) %all-gather.25.cloned.1.call-update) | async-done | bytes 3145744 | tf_op jit(solution)/shard_map/all_gather | solution.py:272
  463.9 88.2 %while.31 = (s32[]{:T(128)}, f32[128,768]{0,1:T(8,128)}, f32[128,768]{0,1:T(8,128)}, f32[128,768]{0,1:T(8,128)}, bf16[2,1024,768]{1,2,0:T(8,128)(2,1)}, /*index=...) while((s32[]{:T(128)}, f32[128,768]{0,1:T(8,128)}, ...), condition=%wide.region_14.15_spmd.clone, body=%wide.region_13.14_spmd.clone.sunk | while | flops 1435501568 | bytes 94612984 | solution.py:59
  477.4 8.7 fusion.167
  499.8 6.3 fusion.164
  521.3 8.7 fusion.167
  530.1 5.1 fusion.166
  543.7 6.3 fusion.164
  572.5 63.3 %reduce-scatter.13.cloned.1.call-done = bf16[96,2304]{1,0:T(8,128)(2,1)} async-done(((bf16[768,2304]{1,0:T(8,128)(2,1)}), bf16[96,2304]{1,0:T(8,128)(2,1)}) %reduce-scatter.13.cloned.1.call-update) | async-done | bytes 442384
  638.0 36.3 %reduce-scatter.7.cloned.1.call-done = bf16[96,768]{1,0:T(8,128)(2,1)} async-done(((bf16[768,768]{1,0:T(8,128)(2,1)}), bf16[96,768]{1,0:T(8,128)(2,1)}) %reduce-scatter.7.cloned.1.call-update) | async-done | bytes 147472 | tf_op jit(solution)/shard_map/reduce_scatter | solution.py:293
  674.4 100.7 %reduce-scatter.11.cloned.1.call-done = bf16[384,768]{1,0:T(8,128)(2,1)} async-done(((bf16[3072,768]{1,0:T(8,128)(2,1)}), bf16[384,768]{1,0:T(8,128)(2,1)}) %reduce-scatter.11.cloned.1.call-update) | async-done | bytes 589840 | tf_op jit(solution)/shard_map/reduce_scatter | solution.py:325
  775.0 101.1 %reduce-scatter.9.cloned.1.call-done = bf16[96,3072]{1,0:T(8,128)(2,1)} async-done(((bf16[768,3072]{1,0:T(8,128)(2,1)}), bf16[96,3072]{1,0:T(8,128)(2,1)}) %reduce-scatter.9.cloned.1.call-update) | async-done | bytes 589840 | tf_op jit(solution)/shard_map/reduce_scatter | solution.py:322
  880.9 29.0 %all-reduce.17 = (bf16[768]{0:T(1024)(128)(2,1)}, bf16[768]{0:T(1024)(128)(2,1)}, bf16[768]{0:T(1024)(128)(2,1)}, bf16[768]{0:T(1024)(128)(2,1)}, bf16[768]{0:T(...) all-reduce(bf16[768]{0:T(1024)(128)(2,1)} %dynamic-update-slice.7, ...), channel_id=1, replica_groups=mesh['seq'=2,'ctx'=4,'fsdp'=4] {'seq','fsdp'}, use_global_device_ids=true, to_apply=%add.7 | all-reduce | flops 9984 | bytes 39936
  920.6 11.0 %all-reduce.19 = (bf16[96]{0:T(256)(128)(2,1)}, bf16[96]{0:T(256)(128)(2,1)}, bf16[96]{0:T(256)(128)(2,1)}, bf16[96]{0:T(256)(128)(2,1)}, bf16[96]{0:T(256)(128)...) all-reduce(bf16[96]{0:T(256)(128)(2,1)} %dynamic-slice.9, ...), channel_id=1, replica_groups=mesh['seq'=2,'ctx'=4,'fsdp'=4] {'ctx'}, use_global_device_ids=true, to_apply=%region_19.20 | all-reduce | flops 1152 | bytes 4608 | tf_op jit(solution)/shard_map/psum | solution.py:315
  (314 shorter events, 185.2 us)
Async XLA Ops:
  7.2 47.8 %all-gather.11.cloned.1.call-start = ((), (), s32[]{:S(2)}) async-start(), calls=%async_computation.4 | async-start | bytes 3981312 | tf_op jit(solution)/shard_map/all_gather | solution.py:88
  7.9 117.8 %all-gather.15.cloned.1.call-start = ((), (), s32[]{:S(2)}) async-start(), calls=%async_computation.6 | async-start | bytes 3342336 | tf_op jit(solution)/shard_map/all_gather | solution.py:146
  58.6 137.1 %all-gather.13.cloned.1.call-start = ((), (), s32[]{:S(2)}) async-start(), calls=%async_computation.5 | async-start | bytes 3342336 | tf_op jit(solution)/shard_map/all_gather | solution.py:145
  59.3 169.0 %all-gather.17.cloned.1.call-start = ((), (), s32[]{:S(2)}) async-start(), calls=%async_computation.7 | async-start | bytes 1327104 | tf_op jit(solution)/shard_map/all_gather | solution.py:89
  59.9 211.3 %all-gather.19.cloned.1.call-start = ((), (), s32[]{:S(2)}) async-start(), calls=%async_computation.8 | async-start | bytes 5308416 | tf_op jit(solution)/shard_map/all_gather | solution.py:165
  60.5 262.7 %all-gather.21.cloned.1.call-start = ((), (), s32[]{:S(2)}) async-start(), calls=%async_computation.9 | async-start | bytes 5308416 | tf_op jit(solution)/shard_map/all_gather | solution.py:166
  61.1 362.5 %all-gather.23.cloned.1.call-start = ((), (), s32[]{:S(2)}) async-start(), calls=%async_computation.10 | async-start | bytes 3342336 | tf_op jit(solution)/shard_map/all_gather | solution.py:269
  100.2 223.0 %copy-start.37 = (f32[768]{0:T(1024)}, f32[768]{0:T(1024)S(1)}, u32[]{:S(2)}) copy-start(f32[768]{0:T(1024)S(1)} %convert_element_type.225) | copy-start | bytes 9220
  122.0 205.6 %copy-start.40 = (f32[768]{0:T(1024)}, f32[768]{0:T(1024)S(1)}, u32[]{:S(2)}) copy-start(f32[768]{0:T(1024)S(1)} %convert_element_type.230) | copy-start | bytes 9220
  122.2 341.7 %all-gather.25.cloned.1.call-start = ((), (), s32[]{:S(2)}) async-start(), calls=%async_computation.11 | async-start | bytes 3342336 | tf_op jit(solution)/shard_map/all_gather | solution.py:272
  228.4 106.7 %copy-start.14 = (f32[128,768]{1,0:T(8,128)}, f32[128,768]{1,0:T(8,128)S(1)}, u32[]{:S(2)}) copy-start(f32[128,768]{1,0:T(8,128)S(1)} %div.37) | copy-start | bytes 1179652
  230.4 103.8 %copy-start.3 = (f32[128,768]{1,0:T(8,128)}, f32[128,768]{1,0:T(8,128)S(1)}, u32[]{:S(2)}) copy-start(f32[128,768]{1,0:T(8,128)S(1)} %get-tuple-element.508) | copy-start | bytes 1179652
  230.5 103.8 %copy-start.42 = (f32[128]{0:T(128)}, f32[128]{0:T(128)S(1)}, u32[]{:S(2)}) copy-start(f32[128]{0:T(128)S(1)} %broadcast_multiply_fusion.5) | copy-start | bytes 1540
  230.7 103.6 %copy-start.44 = (f32[128]{0:T(128)}, f32[128]{0:T(128)S(1)}, u32[]{:S(2)}) copy-start(f32[128]{0:T(128)S(1)} %add_rsqrt_fusion.1) | copy-start | bytes 1540
  336.7 299.0 %reduce-scatter.13.cloned.1.call-start = ((), (), s32[]{:S(2)}) async-start(), calls=%async_computation.15 | async-start | bytes 3981312
  561.2 113.2 %reduce-scatter.7.cloned.1.call-start = ((), (), s32[]{:S(2)}) async-start(), calls=%async_computation.12 | async-start | bytes 1327104 | tf_op jit(solution)/shard_map/reduce_scatter | solution.py:293
  563.8 211.2 %reduce-scatter.11.cloned.1.call-start = ((), (), s32[]{:S(2)}) async-start(), calls=%async_computation.14 | async-start | bytes 5308416 | tf_op jit(solution)/shard_map/reduce_scatter | solution.py:325
  567.5 308.6 %reduce-scatter.9.cloned.1.call-start = ((), (), s32[]{:S(2)}) async-start(), calls=%async_computation.13 | async-start | bytes 5308416 | tf_op jit(solution)/shard_map/reduce_scatter | solution.py:322
  572.4 308.5 %copy-start.48 = (bf16[768]{0:T(1024)(128)(2,1)S(1)}, bf16[768]{0:T(1024)(128)(2,1)}, u32[]{:S(2)}) copy-start(bf16[768]{0:T(1024)(128)(2,1)} %get-tuple-element.390) | copy-start | bytes 4612
  572.4 308.5 %copy-start.49 = (bf16[768]{0:T(1024)(128)(2,1)S(1)}, bf16[768]{0:T(1024)(128)(2,1)}, u32[]{:S(2)}) copy-start(bf16[768]{0:T(1024)(128)(2,1)} %get-tuple-element.483) | copy-start | bytes 4612
  572.4 369.7 %copy-start.41 = (f32[768]{0:T(1024)S(1)}, f32[768]{0:T(1024)}, u32[]{:S(2)}) copy-start(f32[768]{0:T(1024)} %copy-done.40) | copy-start | bytes 9220
  572.5 369.7 %copy-start.47 = (f32[128]{0:T(128)S(1)}, f32[128]{0:T(128)}, u32[]{:S(2)}) copy-start(f32[128]{0:T(128)} %copy-done.46) | copy-start | bytes 1540
  572.5 375.9 %all-reduce.23.cloned.1.call-start = ((), (), s32[]{:S(2)}) async-start(), calls=%async_computation.16 | async-start | bytes 3833856 | tf_op jit(solution)/shard_map/psum | solution.py:313
  635.8 308.2 %copy-start.9 = (bf16[768,2304]{1,0:T(8,128)(2,1)S(1)}, bf16[768,2304]{1,0:T(8,128)(2,1)}, u32[]{:S(2)}) copy-start(bf16[768,2304]{1,0:T(8,128)(2,1)} %all-gather.11.cloned.1.call-done) | copy-start | bytes 10616836
  (54 other events, 349.4 us)
Sparse Core Ops, SparseCore 0:
  9.6 45.3 all-gather.10
  58.7 66.9 all-gather.14
  129.1 66.5 all-gather.12
  197.1 21.1 all-gather.16
  219.7 51.4 all-gather.18
  272.7 50.5 all-gather.20
  326.1 67.1 all-gather.22
  396.1 67.7 all-gather.24
  561.3 74.4 reduce-scatter.12
  638.6 35.7 reduce-scatter.6
  676.8 98.2 reduce-scatter.10
  777.3 98.7 reduce-scatter.8
  880.6 67.7 all-reduce.22
where the time goes:
time: 965 us; the launch traced here: 961 us
  waiting for transfers between devices  504 us (52%)
  blocking collectives  215 us (22%)
  matrix products  109 us (11%)
  local copies, waits for them, and re-layouts  71.5 us (7%)
  other arithmetic  41.4 us (4%)
  between operations  16.9 us (2%)
    reduce_scatter x1, waiting for transfers between devices, shards(): lax.psum_scatter(hidden_grad.astype(jnp.bfloat16), ('seq', 'fsdp'), scatt...  101 us
    reduce_scatter x1, waiting for transfers between devices, shards(): lax.psum_scatter(return_grad.astype(jnp.bfloat16), ('seq', 'fsdp'), scatt...  101 us
    unnamed x14, waiting for transfers between devices  65.7 us
    all_gather x1, waiting for transfers between devices, shards(): lax.all_gather(keys_loc, ('ctx', 'fsdp'), axis=0, tiled=True)  65.3 us
    unnamed x2, blocking collectives  61.4 us
    all_gather x1, waiting for transfers between devices, shards(): lax.all_gather(return_weight, ('seq', 'fsdp'), axis=0, tiled=True)  43.4 us
    all_gather x1, blocking collectives, shards(): lax.all_gather(delta, ('ctx', 'fsdp'), axis=1, tiled=True)  43.1 us
    unnamed x130, local copies, waits for them, and re-layouts  41.6 us
  transfers between devices with their start and end apart: 13, of which 11 were waited for; matrix products, arithmetic and copies ran while one was open for 12% of the time, Pallas kernels for 0%

commit v1 on v0

--- a/solution.py
+++ b/solution.py
@@ -1,12 +1,18 @@
+import functools
 import math
 
 import jax
 import jax.numpy as jnp
 from jax import lax
+from jax.experimental import pallas as pl
+from jax.experimental.pallas import tpu as pltpu
 from jax.sharding import PartitionSpec as P
 
 HEADS = 12
 HEAD_DIM = 64
+MESH = pl.DeviceIdType.MESH
+BF = jnp.bfloat16
+F32 = jnp.float32
 
 
 def contract_rows(operand, other):
@@ -21,14 +27,14 @@
     )
 
 
-def norm_forward(values, gain, shift):
+def any_norm_forward(values, gain, shift):
     center = values - jnp.mean(values, axis=-1, keepdims=True)
     inverse = lax.rsqrt(jnp.mean(center * center, axis=-1, keepdims=True) + 1e-06)
     normed = center * inverse
     return (normed * gain + shift, normed, inverse)
 
 
-def norm_backward(upstream, normed, inverse, gain):
+def any_norm_backward(upstream, normed, inverse, gain):
     gain_grad = jnp.sum(upstream * normed, axis=0)
     shift_grad = jnp.sum(upstream, axis=0)
     scaled = upstream * gain
@@ -62,7 +68,7 @@
     return running
 
 
-def shards(
+def any_shards(
     tokens,
     documents,
     joint_weight,
@@ -156,7 +162,7 @@
     branch = jnp.dot(
         mixed_low, mixer_full, preferred_element_type=jnp.float32
     ) + offset_full.astype(jnp.float32)
-    first_norm, first_hat, first_inv = norm_forward(
+    first_norm, first_hat, first_inv = any_norm_forward(
         inputs.astype(jnp.float32) + branch,
         gain_first.astype(jnp.float32),
         bias_first.astype(jnp.float32),
@@ -180,11 +186,11 @@
         + jnp.dot(acted_low, return_full, preferred_element_type=jnp.float32)
         + outer_shift.astype(jnp.float32)
     )
-    outcome, second_hat, second_inv = norm_forward(
+    outcome, second_hat, second_inv = any_norm_forward(
         second_in, gain_second.astype(jnp.float32), bias_second.astype(jnp.float32)
     )
     upstream = cotangent[0].astype(jnp.float32)
-    back_second, second_scale, second_drift = norm_backward(
+    back_second, second_scale, second_drift = any_norm_backward(
         upstream, second_hat, second_inv, gain_second.astype(jnp.float32)
     )
     back_return = back_second.astype(jnp.bfloat16)
@@ -194,7 +200,7 @@
     hidden_drift = jnp.sum(back_inner.astype(jnp.float32), axis=0)
     hidden_grad = contract_rows(first_low, back_inner)
     back_first = back_second + contract_cols(back_inner, hidden_full)
-    back_first_in, first_scale, first_drift = norm_backward(
+    back_first_in, first_scale, first_drift = any_norm_backward(
         back_first, first_hat, first_inv, gain_first.astype(jnp.float32)
     )
     back_mix = back_first_in.astype(jnp.bfloat16)
@@ -365,44 +371,541 @@
     )
 
 
+T = 128
+C = 512
+HL = 3
+HF = HL * HEAD_DIM
+D = 768
+W3 = 3 * HF
+NEG = -1e30
+
+
+def nn(a, b):
+    return lax.dot_general(a, b, (((1,), (0,)), ((), ())), preferred_element_type=F32)
+
+
+def nt(a, b):
+    return lax.dot_general(a, b, (((1,), (1,)), ((), ())), preferred_element_type=F32)
+
+
+def tn(a, b):
+    return lax.dot_general(a, b, (((0,), (0,)), ((), ())), preferred_element_type=F32)
+
+
+def flip(value, bits):
+    for bit in (1, 2):
+        if bits & bit:
+            value = value + bit - 2 * bit * lax.rem(lax.div(value, bit), 2)
+    return value
+
+
+def places():
+    s, c, z = lax.axis_index("seq"), lax.axis_index("ctx"), lax.axis_index("fsdp")
+    plane = {k: (s, flip(c, k), z) for k in (1, 2, 3)}
+    line = {k: (s, c, flip(z, k)) for k in (1, 2, 3)}
+    return s, c, z, plane, line, (1 - s, c, z)
+
+
+def meet(peers):
+    barrier = pltpu.get_barrier_semaphore()
+    for peer in peers:
+        pl.semaphore_signal(barrier, inc=1, device_id=peer, device_id_type=MESH)
+    pl.semaphore_wait(barrier, len(peers))
+
+
+def push(src, dst, send, recv, index, peer):
+    copy = pltpu.make_async_remote_copy(
+        src_ref=src,
+        dst_ref=dst,
+        send_sem=send.at[index],
+        recv_sem=recv.at[index],
+        device_id=peer,
+        device_id_type=MESH,
+    )
+    copy.start()
+    return copy
+
+
+def split_heads(packed, dest, slot):
+    for part in range(3):
+        for h in range(HL):
+            lo = part * HF + h * HEAD_DIM
+            dest[part][slot, h] = packed[slot, :, lo : lo + HEAD_DIM]
+
+
+def attend_kernel(
+    x_ref, w_ref, doc_ref,
+    mixed_ref, att_ref, lse_ref, xcol_ref, wcol_ref, k_ref, v_ref, q_ref, docs_ref,
+    wbuf, kvq, mix_own, m_sc, l_sc, acc_sc, doc_col,
+    send_x, recv_x, send_w, recv_w, send_d, recv_d, send_c, recv_c, send_kv, recv_kv, send_q, recv_q, send_e, recv_e, send_m, recv_m,
+):
+    s, c, z, plane, line, twin = places()
+    me = 4 * s + z
+    meet([plane[1], plane[2], plane[3], line[1], line[2], line[3], twin])
+    docs_ref[0, z] = doc_ref[...]
+    xcol_ref[pl.ds(pl.multiple_of(z * T, T), T), :] = x_ref[...]
+    mine = xcol_ref.at[pl.ds(pl.multiple_of(z * T, T), T), :]
+    xs = [push(x_ref, mine, send_x, recv_x, k, line[k]) for k in (1, 2, 3)]
+    ds = [push(doc_ref, docs_ref.at[0, z], send_d, recv_d, k, line[k]) for k in (1, 2, 3)]
+    ws = {}
+    for k in (1, 2, 3):
+        ws[k] = push(w_ref.at[flip(z, k)], wbuf.at[me], send_w, recv_w, k, line[k])
+    wbuf[me] = w_ref[z]
+    wt = [push(wbuf.at[me], wbuf.at[me], send_c, recv_c, 0, twin)]
+    for k in (1, 2, 3):
+        ws[k].wait()
+        slot = wbuf.at[4 * s + flip(z, k)]
+        wt.append(push(slot, slot, send_c, recv_c, k, twin))
+    for copy in ds:
+        copy.wait()
+    es = [push(docs_ref.at[0], docs_ref.at[k], send_e, recv_e, k, plane[k]) for k in (1, 2, 3)]
+    for copy in xs:
+        copy.wait()
+    for copy in wt:
+        copy.wait()
+    for i in range(8):
+        wcol_ref[96 * i : 96 * i + 96, :] = wbuf[i, 0:96, :]
+    bias = jnp.zeros((1, W3), F32)
+    for i in range(8):
+        bias = bias + wbuf[i, 96:112, :].astype(F32)[0:1, :]
+    for r in range(2):
+        rows = slice(256 * r, 256 * r + 256)
+        made = nn(xcol_ref[rows, :], wcol_ref[...]) + bias
+        low = made.astype(BF)
+        scaled = (low[:, 2 * HF :].astype(F32) * (1.0 / math.sqrt(HEAD_DIM))).astype(BF)
+        kvq[0, rows, 0 : 2 * HF] = low[:, 0 : 2 * HF]
+        kvq[0, rows, 2 * HF : W3] = scaled
+        kvq[0, rows, W3:] = jnp.zeros((256, 640 - W3), BF)
+    kvs = [push(kvq.at[0, :, 0 : 2 * HF], kvq.at[k, :, 0 : 2 * HF], send_kv, recv_kv, k, plane[k]) for k in (1, 2, 3)]
+    qs = [push(kvq.at[0, :, 2 * HF :], kvq.at[k, :, 2 * HF :], send_q, recv_q, k, plane[k]) for k in (1, 2, 3)]
+    split_heads(kvq, (k_ref, v_ref, q_ref), 0)
+    for j in range(4):
+        row = docs_ref[0, j, 0:1, :].astype(F32)
+        doc_col[128 * j : 128 * j + 128, :] = jnp.transpose(jnp.broadcast_to(row, (T, T)))
+    m_sc[...] = jnp.full(m_sc.shape, NEG, F32)
+    l_sc[...] = jnp.zeros(l_sc.shape, F32)
+    acc_sc[...] = jnp.zeros(acc_sc.shape, F32)
+    for k in range(4):
+        if k:
+            es[k - 1].wait()
+            kvs[k - 1].wait()
+            for part, dest in enumerate((k_ref, v_ref)):
+                for h in range(HL):
+                    lo = part * HF + h * HEAD_DIM
+                    dest[k, h] = kvq[k, :, lo : lo + HEAD_DIM]
+        keys_doc = jnp.concatenate([docs_ref[k, j, 0:1, :] for j in range(4)], axis=1).astype(F32)
+
+        def one(step, carry, k=k, keys_doc=keys_doc):
+            h = lax.div(step, 2)
+            rows = pl.ds(pl.multiple_of(lax.rem(step, 2) * 256, 256), 256)
+            scores = nt(q_ref[0, h, rows, :], k_ref[k, h])
+            allowed = doc_col[rows, 0:1] == keys_doc
+            masked = jnp.where(allowed, scores, NEG)
+            old = m_sc[h, rows, 0:1]
+            new = jnp.maximum(old, jnp.max(masked, axis=1, keepdims=True))
+            weights = jnp.where(allowed, jnp.exp(masked - new), 0.0)
+            fade = jnp.exp(old - new)
+            m_sc[h, rows, 0:1] = new
+            l_sc[h, rows, 0:1] = l_sc[h, rows, 0:1] * fade + jnp.sum(weights, axis=1, keepdims=True)
+            acc_sc[h, rows, :] = acc_sc[h, rows, :] * fade + nn(weights.astype(BF), v_ref[k, h])
+            return carry
+
+        lax.fori_loop(0, 2 * HL, one, 0)
+    lane = lax.broadcasted_iota(jnp.int32, (C, T), 1)
+    stats = jnp.zeros((C, T), F32)
+    for h in range(HL):
+        total = l_sc[h, :, 0:1]
+        part = acc_sc[h] / total
+        att_ref[:, h * HEAD_DIM : (h + 1) * HEAD_DIM] = part
+        mix_own[:, h * HEAD_DIM : (h + 1) * HEAD_DIM] = part.astype(BF)
+        stats = jnp.where(lane == h, m_sc[h, :, 0:1] + jnp.log(total), stats)
+    lse_ref[...] = stats
+    ms = []
+    for k in (1, 2, 3):
+        rows = pl.ds(pl.multiple_of(flip(z, k) * T, T), T)
+        ms.append(push(mix_own.at[rows, :], mixed_ref.at[z], send_m, recv_m, k, line[k]))
+    mixed_ref[z] = mix_own[pl.ds(pl.multiple_of(z * T, T), T), :]
+    for k in (1, 2, 3):
+        qs[k - 1].wait()
+        for h in range(HL):
+            lo = 2 * HF + h * HEAD_DIM
+            q_ref[k, h] = kvq[k, :, lo : lo + HEAD_DIM]
+    for copy in ms:
+        copy.wait()
+
+
+def attend(x, w_parts, doc_rows):
+    heads = jax.ShapeDtypeStruct((4, HL, C, HEAD_DIM), BF)
+    vmem = pl.BlockSpec(memory_space=pltpu.VMEM)
+    dma = pltpu.SemaphoreType.DMA((4,))
+    return pl.pallas_call(
+        attend_kernel,
+        out_shape=(
+            jax.ShapeDtypeStruct((4, T, HF), BF),
+            jax.ShapeDtypeStruct((C, HF), F32),
+            jax.ShapeDtypeStruct((C, T), F32),
+            jax.ShapeDtypeStruct((C, D), BF),
+            jax.ShapeDtypeStruct((D, W3), BF),
+            heads,
+            heads,
+            heads,
+            jax.ShapeDtypeStruct((4, 4, 8, T), jnp.int32),
+        ),
+        in_specs=[vmem] * 3,
+        out_specs=(vmem,) * 9,
+        scratch_shapes=[
+            pltpu.VMEM((8, 112, W3), BF),
+            pltpu.VMEM((4, C, 640), BF),
+            pltpu.VMEM((C, HF), BF),
+            pltpu.VMEM((HL, C, 128), F32),
+            pltpu.VMEM((HL, C, 128), F32),
+            pltpu.VMEM((HL, C, HEAD_DIM), F32),
+            pltpu.VMEM((C, T), F32),
+        ]
+        + [dma] * 16,
+        compiler_params=pltpu.CompilerParams(
+            collective_id=0, has_side_effects=True, vmem_limit_bytes=50 << 20
+        ),
+        cost_estimate=pl.CostEstimate(flops=40_000_000_000, bytes_accessed=20_000_000, transcendentals=4_000_000),
+    )(x, w_parts, doc_rows)
+
+
+def norm_forward(values, gain, shift):
+    center = values - jnp.mean(values, axis=-1, keepdims=True)
+    inverse = lax.rsqrt(jnp.mean(center * center, axis=-1, keepdims=True) + 1e-06)
+    normed = center * inverse
+    return (normed * gain + shift, normed, inverse)
+
+
+def norm_backward(upstream, normed, inverse, gain):
+    scaled = upstream * gain
+    plain_mean = jnp.mean(scaled, axis=-1, keepdims=True)
+    cross_mean = jnp.mean(scaled * normed, axis=-1, keepdims=True)
+    return inverse * (scaled - plain_mean - normed * cross_mean)
+
+
+def total_rows(values):
+    return jnp.sum(values, axis=0, keepdims=True)
+
+
+MIXER_BIAS, FIRST_GAIN, FIRST_BIAS, RETURN_BIAS, SECOND_GAIN, SECOND_BIAS, HIDDEN_BIAS = range(7)
+
+
+def dense_kernel(
+    x_ref, mixed_ref, mixer_ref, hid_ref, ret_ref, small_ref, cot_ref,
+    out_ref, bfi_ref, datt_ref, rgrad_ref, hgrad_ref, mgrad_ref, vec_ref,
+    firsts, acted, slope, sent, parts, backs, inners, datt_own,
+    send_f, recv_f, send_p, recv_p, send_r, recv_r, send_b, recv_b, send_a, recv_a,
+):
+    s, c, z, plane, line, twin = places()
+    meet([plane[1], plane[2], plane[3], line[1], line[2], line[3]])
+
+    def small(row):
+        return small_ref[row : row + 1, :]
+
+    branch = small(MIXER_BIAS)
+    for j in range(4):
+        branch = branch + nn(mixed_ref[j], mixer_ref[HF * j : HF * j + HF, :])
+    first, hat1, inv1 = norm_forward(x_ref[...].astype(F32) + branch, small(FIRST_GAIN), small(FIRST_BIAS))
+    firsts[0:T, :] = first.astype(BF)
+    fs = [push(firsts.at[0:T, :], firsts.at[T * k : T * k + T, :], send_f, recv_f, k, plane[k]) for k in (1, 2, 3)]
+    ps = []
+    second_in = first + small(RETURN_BIAS)
+    for k in range(4):
+        rows = slice(T * k, T * k + T)
+        if k:
+            fs[k - 1].wait()
+        inner = nn(firsts[rows, :], hid_ref[...]) + small(HIDDEN_BIAS)
+        phi = 0.5 * (1.0 + lax.erf(inner * math.sqrt(0.5)))
+        slope[rows, :] = phi + inner * (jnp.exp(-0.5 * inner * inner) * (1.0 / math.sqrt(2.0 * math.pi)))
+        acted[rows, :] = (inner * phi).astype(BF)
+        made = nn(acted[rows, :], ret_ref[...])
+        if k:
+            sent[k] = made.astype(BF)
+            ps.append(push(sent.at[k], parts.at[k], send_p, recv_p, k, plane[k]))
+        else:
+            second_in = second_in + made
+    for k in (1, 2, 3):
+        ps[k - 1].wait()
+        second_in = second_in + parts[k].astype(F32)
+    outcome, hat2, inv2 = norm_forward(second_in, small(SECOND_GAIN), small(SECOND_BIAS))
+    upstream = cot_ref[...].astype(F32)
+    back_second = norm_backward(upstream, hat2, inv2, small(SECOND_GAIN))
+    backs[0:T, :] = back_second.astype(BF)
+    rs = [push(backs.at[0:T, :], backs.at[T * k : T * k + T, :], send_r, recv_r, k, plane[k]) for k in (1, 2, 3)]
+    out_ref[...] = outcome.astype(BF)
+    vec_ref[0:1, :] = total_rows(upstream * hat2)
+    vec_ref[1:2, :] = total_rows(upstream)
+    vec_ref[2:3, :] = total_rows(backs[0:T, :].astype(F32))
+    back_first = back_second
+    hidden_drift = jnp.zeros((1, D), F32)
+    bs = []
+    for k in range(4):
+        rows = slice(T * k, T * k + T)
+        if k:
+            rs[k - 1].wait()
+        pulled = (nt(backs[rows, :], ret_ref[...]) * slope[rows, :]).astype(BF)
+        inners[rows, :] = pulled
+        hidden_drift = hidden_drift + total_rows(pulled.astype(F32))
+        made = nt(pulled, hid_ref[...])
+        if k:
+            sent[k] = made.astype(BF)
+            bs.append(push(sent.at[k], parts.at[4 + k], send_b, recv_b, k, plane[k]))
+        else:
+            back_first = back_first + made
+    rgrad_ref[...] = tn(acted[...], backs[...]).astype(BF)
+    hgrad_ref[...] = tn(firsts[...], inners[...]).astype(BF)
+    for k in (1, 2, 3):
+        bs[k - 1].wait()
+        back_first = back_first + parts[4 + k].astype(F32)
+    back_first_in = norm_backward(back_first, hat1, inv1, small(FIRST_GAIN))
+    back_mix = back_first_in.astype(BF)
+    for j in range(4):
+        datt_own[j] = nt(back_mix, mixer_ref[HF * j : HF * j + HF, :]).astype(BF)
+    as_ = [push(datt_own.at[flip(z, k)], datt_ref.at[z], send_a, recv_a, k, line[k]) for k in (1, 2, 3)]
+    datt_ref[z] = datt_own[z]
+    bfi_ref[...] = back_first_in
+    for j in range(4):
+        mgrad_ref[HF * j : HF * j + HF, :] = tn(mixed_ref[j], back_mix).astype(BF)
+    vec_ref[3:4, :] = total_rows(back_first * hat1)
+    vec_ref[4:5, :] = total_rows(back_first)
+    vec_ref[5:6, :] = total_rows(back_mix.astype(F32))
+    vec_ref[6:7, :] = hidden_drift
+    vec_ref[7:8, :] = jnp.zeros((1, D), F32)
+    for copy in as_:
+        copy.wait()
+
+
+def dense(x, mixed, mixer, hid, ret, small, cot):
+    vmem = pl.BlockSpec(memory_space=pltpu.VMEM)
+    dma = pltpu.SemaphoreType.DMA((4,))
+    square = jax.ShapeDtypeStruct((D, D), BF)
+    return pl.pallas_call(
+        dense_kernel,
+        out_shape=(
+            jax.ShapeDtypeStruct((T, D), BF),
+            jax.ShapeDtypeStruct((T, D), F32),
+            jax.ShapeDtypeStruct((4, T, HF), BF),
+            square,
+            square,
+            square,
+            jax.ShapeDtypeStruct((8, D), F32),
+        ),
+        in_specs=[vmem] * 7,
+        out_specs=(vmem,) * 7,
+        scratch_shapes=[
+            pltpu.VMEM((4 * T, D), BF),
+            pltpu.VMEM((4 * T, D), BF),
+            pltpu.VMEM((4 * T, D), F32),
+            pltpu.VMEM((4, T, D), BF),
+            pltpu.VMEM((8, T, D), BF),
+            pltpu.VMEM((4 * T, D), BF),
+            pltpu.VMEM((4 * T, D), BF),
+            pltpu.VMEM((4, T, HF), BF),
+        ]
+        + [dma] * 10,
+        compiler_params=pltpu.CompilerParams(
+            collective_id=1, has_side_effects=True, vmem_limit_bytes=50 << 20
+        ),
+        cost_estimate=pl.CostEstimate(flops=30_000_000_000, bytes_accessed=10_000_000, transcendentals=1_000_000),
+    )(x, mixed, mixer, hid, ret, small, cot)
+
+
+def pull_kernel(
+    datt_ref, att_ref, lse_ref, k_ref, v_ref, q_ref, docs_ref, xcol_ref, wcol_ref, bfi_ref,
+    tok_ref, jgrad_ref, qv_ref,
+    d_own, d_all, stat, dcol, dheads, doc_col, dq, dk, dv, packed, sent, parts,
+    send_d, recv_d, send_s, recv_s, send_t, recv_t,
+):
+    s, c, z, plane, line, twin = places()
+    meet([plane[1], plane[2], plane[3], line[1], line[2], line[3]])
+    for j in range(4):
+        d_own[T * j : T * j + T, 0:HF] = datt_ref[j]
+        row = docs_ref[0, j, 0:1, :].astype(F32)
+        doc_col[128 * j : 128 * j + 128, :] = jnp.transpose(jnp.broadcast_to(row, (T, T)))
+    ds = [push(d_own, d_all.at[k], send_d, recv_d, k, plane[k]) for k in (1, 2, 3)]
+    lane = lax.broadcasted_iota(jnp.int32, (C, T), 1)
+    stats = jnp.where(lane < HL, lse_ref[...], 0.0)
+    for h in range(HL):
+        cols = slice(h * HEAD_DIM, (h + 1) * HEAD_DIM)
+        dheads[0, h] = d_own[:, cols]
+        delta = jnp.sum(d_own[:, cols].astype(F32) * att_ref[:, cols], axis=1, keepdims=True)
+        stats = jnp.where(lane == 4 + h, delta, stats)
+    dcol[...] = stats
+    stat[0] = jnp.transpose(stats)[0:8, :]
+    ss = [push(stat.at[0], stat.at[k], send_s, recv_s, k, plane[k]) for k in (1, 2, 3)]
+    dq[...] = jnp.zeros(dq.shape, F32)
+    dk[...] = jnp.zeros(dk.shape, F32)
+    dv[...] = jnp.zeros(dv.shape, F32)
+
+    def doc_row(k):
+        return jnp.concatenate([docs_ref[k, j, 0:1, :] for j in range(4)], axis=1).astype(F32)
+
+    for k in range(4):
+        keys_doc = doc_row(k)
+
+        def one(step, carry, k=k, keys_doc=keys_doc):
+            h = lax.div(step, 2)
+            rows = pl.ds(pl.multiple_of(lax.rem(step, 2) * 256, 256), 256)
+            scores = nt(q_ref[0, h, rows, :], k_ref[k, h])
+            allowed = doc_col[rows, 0:1] == keys_doc
+            lanes = lax.broadcasted_iota(jnp.int32, (256, T), 1)
+            both = dcol[rows, :]
+            lse = jnp.sum(jnp.where(lanes == h, both, 0.0), axis=1, keepdims=True)
+            delta = jnp.sum(jnp.where(lanes == 4 + h, both, 0.0), axis=1, keepdims=True)
+            probs = jnp.where(allowed, jnp.exp(scores - lse), 0.0)
+            dprobs = nt(dheads[0, h, rows, :], v_ref[k, h])
+            dscores = (probs * (dprobs - delta)).astype(BF)
+            dq[h, rows, :] = dq[h, rows, :] + nn(dscores, k_ref[k, h])
+            return carry
+
+        lax.fori_loop(0, 2 * HL, one, 0)
+    for k in range(4):
+        if k:
+            ds[k - 1].wait()
+            ss[k - 1].wait()
+            for h in range(HL):
+                dheads[k, h] = d_all[k, :, h * HEAD_DIM : (h + 1) * HEAD_DIM]
+        query_doc = doc_row(k)
+
+        def other(step, carry, k=k, query_doc=query_doc):
+            h = lax.div(step, 2)
+            rows = pl.ds(pl.multiple_of(lax.rem(step, 2) * 256, 256), 256)
+            scores = nt(k_ref[0, h, rows, :], q_ref[k, h])
+            allowed = doc_col[rows, 0:1] == query_doc
+            probs = jnp.where(allowed, jnp.exp(scores - stat[k, pl.ds(h, 1), :]), 0.0)
+            dv[h, rows, :] = dv[h, rows, :] + nn(probs.astype(BF), dheads[k, h])
+            dprobs = nt(v_ref[0, h, rows, :], dheads[k, h])
+            dscores = (probs * (dprobs - stat[k, pl.ds(4 + h, 1), :])).astype(BF)
+            dk[h, rows, :] = dk[h, rows, :] + nn(dscores, q_ref[k, h])
+            return carry
+
+        lax.fori_loop(0, 2 * HL, other, 0)
+    for h in range(HL):
+        lo = h * HEAD_DIM
+        packed[:, lo : lo + HEAD_DIM] = dk[h].astype(BF)
+        packed[:, HF + lo : HF + lo + HEAD_DIM] = dv[h].astype(BF)
+        packed[:, 2 * HF + lo : 2 * HF + lo + HEAD_DIM] = (dq[h] * (1.0 / math.sqrt(HEAD_DIM))).astype(BF)
+    ts = []
+    for j in range(4):
+        sent[j] = nt(packed[T * j : T * j + T, :], wcol_ref[...]).astype(BF)
+    for k in (1, 2, 3):
+        ts.append(push(sent.at[flip(z, k)], parts.at[k], send_t, recv_t, k, line[k]))
+    jgrad_ref[...] = tn(xcol_ref[...], packed[...]).astype(BF)
+    qv_ref[...] = jnp.broadcast_to(total_rows(packed[...].astype(F32)), (8, W3))
+    rows = pl.ds(pl.multiple_of(z * T, T), T)
+    made = bfi_ref[...] + nt(packed[rows, :], wcol_ref[...])
+    for k in (1, 2, 3):
+        ts[k - 1].wait()
+        made = made + parts[k].astype(F32)
+    tok_ref[...] = made
+
+
+def pull(datt, att, lse, keys, values, queries, docs, xcol, wcol, bfi):
+    vmem = pl.BlockSpec(memory_space=pltpu.VMEM)
+    dma = pltpu.SemaphoreType.DMA((4,))
+    grads = pltpu.VMEM((HL, C, HEAD_DIM), F32)
+    return pl.pallas_call(
+        pull_kernel,
+        out_shape=(
+            jax.ShapeDtypeStruct((T, D), F32),
+            jax.ShapeDtypeStruct((D, W3), BF),
+            jax.ShapeDtypeStruct((8, W3), F32),
+        ),
+        in_specs=[vmem] * 10,
+        out_specs=(vmem,) * 3,
+        scratch_shapes=[
+            pltpu.VMEM((C, 256), BF),
+            pltpu.VMEM((4, C, 256), BF),
+            pltpu.VMEM((4, 8, C), F32),
+            pltpu.VMEM((C, T), F32),
+            pltpu.VMEM((4, HL, C, HEAD_DIM), BF),
+            pltpu.VMEM((C, T), F32),
+            grads,
+            grads,
+            grads,
+            pltpu.VMEM((C, W3), BF),
+            pltpu.VMEM((4, T, D), BF),
+            pltpu.VMEM((4, T, D), BF),
+        ]
+        + [dma] * 6,
+        compiler_params=pltpu.CompilerParams(
+            collective_id=2, has_side_effects=True, vmem_limit_bytes=50 << 20
+        ),
+        cost_estimate=pl.CostEstimate(flops=60_000_000_000, bytes_accessed=10_000_000, transcendentals=8_000_000),
+    )(datt, att, lse, keys, values, queries, docs, xcol, wcol, bfi)
+
+
+def shards(
+    tokens, documents, joint_weight, query_bias, value_bias, mixer_weight, mixer_bias, first_gain, first_bias,
+    hidden_weight, hidden_bias, return_weight, return_bias, second_gain, second_bias, cotangent,
+):
+    s, c, z = lax.axis_index("seq"), lax.axis_index("ctx"), lax.axis_index("fsdp")
+    me = 4 * s + z
+    x = tokens[0]
+    cols = joint_weight.reshape(96, 3, 4, HF)
+    cols = jnp.stack([cols[:, 1], cols[:, 2], cols[:, 0]], axis=2)
+    cols = cols.transpose(1, 0, 2, 3).reshape(4, 96, W3)
+    place = (jnp.arange(8, dtype=jnp.int32) == me).astype(BF)
+    vals = (place[:, None] * value_bias[None, :]).reshape(4, 1, HF)
+    qrys = (place[:, None] * query_bias[None, :]).reshape(4, 1, HF)
+    bias = jnp.concatenate([jnp.zeros((4, 1, HF), BF), vals, qrys], axis=2)
+    w_parts = jnp.concatenate([cols, bias, jnp.zeros((4, 15, W3), BF)], axis=1)
+    doc_rows = jnp.broadcast_to(documents, (8, T))
+    hid_part = lax.dynamic_index_in_dim(hidden_weight.reshape(96, 8, 4, 96), c, 2, keepdims=False).reshape(96, D)
+    ret_part = lax.dynamic_slice_in_dim(return_weight, 96 * c, 96, 0)
+    hb_part = lax.dynamic_slice_in_dim(hidden_bias, 96 * c, 96, 0)
+    smalls = jnp.stack([mixer_bias, first_gain, first_bias, return_bias, second_gain, second_bias, hb_part, hb_part])
+    gather = functools.partial(lax.all_gather, axis_name=("seq", "fsdp"))
+    mixer_full = gather(mixer_weight, axis=0, tiled=True)
+    hid_full = gather(hid_part, axis=0, tiled=True)
+    ret_full = gather(ret_part, axis=0, tiled=True)
+    small_full = gather(smalls, axis=1, tiled=True).astype(F32)
+
+    mixed, att, lse, xcol, wcol, keys, values, queries, docs = attend(x, w_parts, doc_rows)
+    outcome, bfi, datt, rgrad, hgrad, mgrad, vecs = dense(
+        x, mixed, mixer_full, hid_full, ret_full, small_full, cotangent[0]
+    )
+    tok, jgrad, qv = pull(datt, att, lse, keys, values, queries, docs, xcol, wcol, bfi)
+
+    scatter = functools.partial(lax.psum_scatter, axis_name=("seq", "fsdp"), scatter_dimension=0, tiled=True)
+    ret_sum = lax.all_gather(scatter(rgrad), "ctx", axis=0, tiled=True).astype(F32)
+    hid_sum = lax.all_gather(scatter(hgrad).reshape(96, 8, 1, 96), "ctx", axis=2, tiled=True)
+    hid_sum = hid_sum.astype(F32).reshape(96, 4 * D)
+    mixer_sum = lax.psum(scatter(mgrad), "ctx").astype(F32)
+    wide = jnp.zeros((4, D, W3), BF)
+    wide = lax.dynamic_update_index_in_dim(wide, jgrad, z, 0)
+    wide = wide.reshape(4, D, 3, HF).transpose(1, 2, 0, 3)
+    wide = jnp.stack([wide[:, 2], wide[:, 0], wide[:, 1]], axis=1).reshape(D, 3 * D)
+    joint_sum = lax.psum(scatter(wide), "ctx").astype(F32)
+    sums = lax.psum(vecs, ("seq", "ctx", "fsdp"))
+    drift = lax.psum(vecs[6], ("seq", "fsdp")).reshape(8, 96)
+    drift = lax.all_gather(lax.dynamic_index_in_dim(drift, me, 0, keepdims=False), "ctx", axis=0, tiled=True)
+    both = jnp.zeros((4, 2, HF), F32)
+    both = lax.dynamic_update_index_in_dim(both, qv[0].reshape(3, HF)[1:3], z, 0)
+    both = lax.psum(both, ("seq", "ctx", "fsdp"))
+    own = lambda vector: lax.dynamic_slice_in_dim(vector.reshape(-1), 96 * me, 96, 0)
+    return (
+        outcome[None], tok[None], joint_sum, own(both[:, 1]), own(both[:, 0]), mixer_sum, own(sums[5]), own(sums[3]),
+        own(sums[4]), hid_sum, drift, ret_sum, own(sums[2]), own(sums[0]), own(sums[1]),
+    )
+
+
+def specs():
+    rows, flat = P(("seq", "fsdp"), None), P(("seq", "fsdp"))
+    toks, docs = P("seq", ("ctx", "fsdp"), None), P("seq", ("ctx", "fsdp"))
+    ins = (
+        toks, docs, rows, flat, flat, rows, flat, flat, flat, rows, flat, rows, flat, flat, flat, toks,
+    )
+    outs = (
+        toks, toks, rows, flat, flat, rows, flat, flat, flat, rows, flat, rows, flat, flat, flat,
+    )
+    return ins, outs
+
+
 def solution(mesh):
+    ins, outs = specs()
+    small_slice = mesh.shape["ctx"] == 4 and mesh.shape["fsdp"] == 4 and mesh.shape["seq"] == 2
     return jax.shard_map(
-        shards,
-        mesh=mesh,
-        in_specs=(
-            P("seq", ("ctx", "fsdp"), None),
-            P("seq", ("ctx", "fsdp")),
-            P(("seq", "fsdp"), None),
-            P(("seq", "fsdp")),
-            P(("seq", "fsdp")),
-            P(("seq", "fsdp"), None),
-            P(("seq", "fsdp")),
-            P(("seq", "fsdp")),
-            P(("seq", "fsdp")),
-            P(("seq", "fsdp"), None),
-            P(("seq", "fsdp")),
-            P(("seq", "fsdp"), None),
-            P(("seq", "fsdp")),
-            P(("seq", "fsdp")),
-            P(("seq", "fsdp")),
-            P("seq", ("ctx", "fsdp"), None),
-        ),
-        out_specs=(
-            P("seq", ("ctx", "fsdp"), None),
-            P("seq", ("ctx", "fsdp"), None),
-            P(("seq", "fsdp"), None),
-            P(("seq", "fsdp")),
-            P(("seq", "fsdp")),
-            P(("seq", "fsdp"), None),
-            P(("seq", "fsdp")),
-            P(("seq", "fsdp")),
-            P(("seq", "fsdp")),
-            P(("seq", "fsdp"), None),
-            P(("seq", "fsdp")),
-            P(("seq", "fsdp"), None),
-            P(("seq", "fsdp")),
-            P(("seq", "fsdp")),
-            P(("seq", "fsdp")),
-        ),
-        check_vma=False,
-    )
+        shards if small_slice else any_shards, mesh=mesh, in_specs=ins, out_specs=outs, check_vma=False
+    )

time: 965 us -> 483 us (0.50)
  waiting for transfers between devices: 504 us -> 132 us
  Pallas kernels: 0 us -> 175 us
  matrix products: 109 us -> 0 us
  blocking collectives: 215 us -> 121 us
  other arithmetic: 41.4 us -> 2.45 us
  local copies, waits for them, and re-layouts: 71.5 us -> 36.2 us
    all_gather x8 -> x3, waiting for transfers between devices: 200 us -> 0.01 us  [the longest x1 0.01 us: shards(): ret_full = gather(ret_part, axis=0, tiled=True)]
    pallas_call x0 -> x3, Pallas kernels: none -> 175 us  [the longest x1 79.5 us: attend(): pl.pallas_call(attend_kernel, out_shape=(jax.ShapeDtypeStruct((4, T, HF),...]
    reduce_scatter x3, waiting for transfers between devices: 238 us -> 80.7 us  [the longest x1 36 us: shards(): mixer_sum = lax.psum(scatter(mgrad), 'ctx').astype(F32)]
    dot_general x26 -> x0, matrix products: 109 us -> none  [the longest x2 17.5 us: backward_step(): jnp.einsum('hqk,qhd->khd', dscores_rev, query_split, preferred_element_ty...]
    all_gather x4, blocking collectives: 143 us -> 59.7 us  [the longest x1 22.9 us: shards(): small_full = gather(smalls, axis=1, tiled=True).astype(F32)]
    unnamed x2 -> x0, blocking collectives: 61.4 us -> none
    unnamed x14 -> x9, waiting for transfers between devices: 65.7 us -> 14 us
    psum x1 -> x2, blocking collectives: 11 us -> 61.3 us  [the longest x1 44.5 us: shards(): both = lax.psum(both, ('seq', 'ctx', 'fsdp'))]
  transfers between devices with their start and end apart: 13 -> 8, of which waited for: 11 -> 5; matrix products, arithmetic and copies ran while one was open for 12% -> 4% of each run, Pallas kernels for 0% -> 16%
where the time goes in v1:
time: 483 us; the launch traced here: 482 us
  Pallas kernels  175 us (36%)
  waiting for transfers between devices  132 us (27%)
  blocking collectives  121 us (25%)
  local copies, waits for them, and re-layouts  36.2 us (7%)
  between operations  15.3 us (3%)
    pallas_call x1, Pallas kernels, attend(): pl.pallas_call(attend_kernel, out_shape=(jax.ShapeDtypeStruct((4, T, HF),...  79.5 us
    pallas_call x1, Pallas kernels, dense(): pl.pallas_call(dense_kernel, out_shape=(jax.ShapeDtypeStruct((T, D), BF),...  49.9 us
    pallas_call x1, Pallas kernels, pull(): pl.pallas_call(pull_kernel, out_shape=(jax.ShapeDtypeStruct((T, D), F32),...  45.8 us
    psum x1, blocking collectives, shards(): both = lax.psum(both, ('seq', 'ctx', 'fsdp'))  44.5 us
    psum x1, waiting for transfers between devices, shards(): joint_sum = lax.psum(scatter(wide), 'ctx').astype(F32)  37.4 us
    reduce_scatter x1, waiting for transfers between devices, shards(): mixer_sum = lax.psum(scatter(mgrad), 'ctx').astype(F32)  36 us
    reduce_scatter x1, waiting for transfers between devices, shards(): scatter(hgrad).reshape(96, 8, 1, 96)  24.4 us
    all_gather x1, blocking collectives, shards(): small_full = gather(smalls, axis=1, tiled=True).astype(F32)  22.9 us
  transfers between devices with their start and end apart: 8, of which 5 were waited for; matrix products, arithmetic and copies ran while one was open for 4% of the time, Pallas kernels for 16%

profile of v1, /device:TPU:0, one launch (start us, length us, event | category | flops | bytes accessed | tf_op | source)
XLA Modules:
  0.0 482.4 jit_solution(3386957612994110329)
XLA Ops:
  9.0 2.3 reshape.158
  11.4 1.2 dynamic-slice_reduce_fusion
  16.6 22.9 %all-gather.1 = bf16[8,96,8]{1,2,0:T(8,128)(2,1)S(1)} all-gather(bf16[1,96,8]{1,2,0:T(8,128)(2,1)S(1)} %bitcast.64), channel_id=1, replica_groups=mesh['seq'=2,'ctx'=4,'fsdp'=4] {'seq','fsdp'}, dimensions={0}, use_global_device_ids=true | all-gather | bytes 13824 | tf_op jit(solution)/shard_map/all_gather | solution.py:863
  39.9 79.5 %shard_map.271 = (bf16[4,128,192]{2,1,0:T(8,128)(2,1)S(1)}, f32[512,192]{1,0:T(8,128)S(1)}, f32[512,128]{1,0:T(8,128)S(1)}, bf16[512,768]{1,0:T(8,128)(2,1)S(1)}...) custom-call(bf16[128,768]{1,0:T(8,128)(2,1)S(1)} %bitcast.56, ...), custom_call_target="tpu_custom_call" | custom-call | flops 40000000000 | bytes 20000000 | tf_op jit(solution)/shard_map/pallas_call | solution.py:541
  121.0 49.9 %shard_map.272 = (bf16[128,768]{1,0:T(8,128)(2,1)S(1)}, f32[128,768]{1,0:T(8,128)S(1)}, bf16[4,128,192]{2,1,0:T(8,128)(2,1)S(1)}, bf16[768,768]{1,0:T(8,128)(2,1...) custom-call(bf16[128,768]{1,0:T(8,128)(2,1)S(1)} %bitcast.57, ...), custom_call_target="tpu_custom_call" | custom-call | flops 30000001024 | bytes 10000000 | tf_op jit(solution)/shard_map/pallas_call | solution.py:683
  171.8 45.8 %shard_map.273 = (f32[128,768]{1,0:T(8,128)S(1)}, bf16[768,576]{1,0:T(8,128)(2,1)S(1)}, f32[8,576]{1,0:T(8,128)S(1)}) custom-call(bf16[4,128,192]{2,1,0:T(8,128)(2,1)S(1)} %get-tuple-element.36.datt_ref, f32[512,192]{1,0:T(8,128)S(1)} %get-tuple-element.37.att_ref, f32[512,128]{1,0:T(8,128)S(1)} %copy-done.5, ...), custom_call_target="tpu_custom_call" | custom-call | flops 60000002048 | bytes 10000000 | tf_op jit(solution)/shard_map/pallas_call | solution.py:808
  219.1 2.1 copy.82
  221.2 5.8 %copy.85 = bf16[768,2304]{1,0:T(8,128)(2,1)} copy(bf16[768,2304]{0,1:T(8,128)(2,1)} %bitcast.59) | data formatting | bytes 7077888
  230.5 44.5 %all-reduce.1 = (f32[4,2,192]{2,1,0:T(2,128)S(1)}, f32[8,768]{1,0:T(8,128)S(1)}) all-reduce(f32[4,2,192]{2,1,0:T(2,128)S(1)} %constant_dynamic-update-slice_fusion, f32[8,768]{1,0:T(8,128)S(1)} %get-tuple-element.50), channel_id=1, replica_groups=mesh['seq'=2,'ctx'=4,'fsdp'=4] {'seq','ctx','fsdp'}, use_global_device_ids=true, to_apply=%region_2.3 | all-reduce | flops 7680 | bytes 61440 | tf_op jit(solution)/shard_map/psum | solution.py:886
  275.0 16.8 %psum.39 = f32[8,96]{1,0:T(8,128)S(1)} all-reduce(f32[8,96]{1,0:T(8,128)S(1)} %reshape.165), channel_id=1, replica_groups=mesh['seq'=2,'ctx'=4,'fsdp'=4] {'seq','fsdp'}, use_global_device_ids=true, to_apply=%region_7.8 | all-reduce | flops 768 | bytes 6144 | tf_op jit(solution)/shard_map/psum | solution.py:882
  293.6 11.5 %reduce-scatter.13.cloned.1.call-done = bf16[96,2304]{1,0:T(8,128)(2,1)} async-done(((bf16[768,2304]{1,0:T(8,128)(2,1)}), bf16[96,2304]{1,0:T(8,128)(2,1)}) %reduce-scatter.13.cloned.1.call-update) | async-done | bytes 442384
  305.1 2.1 copy.86
  307.2 36.0 %reduce-scatter.7.cloned.1.call-done = bf16[96,768]{1,0:T(8,128)(2,1)} async-done(((bf16[768,768]{1,0:T(8,128)(2,1)}), bf16[96,768]{1,0:T(8,128)(2,1)}) %reduce-scatter.7.cloned.1.call-update) | async-done | bytes 147472 | tf_op jit(solution)/shard_map/reduce_scatter | solution.py:875
  344.7 10.2 %all-reduce = f32[384]{0:T(512)} all-reduce(f32[384]{0:T(512)S(1)} %fusion.5), channel_id=2, replica_groups=mesh['seq'=2,'ctx'=4,'fsdp'=4] {'ctx'}, use_global_device_ids=true, to_apply=%add | all-reduce | flops 384 | bytes 3072 | tf_op jit(solution)/shard_map/all_gather | solution.py:883
  356.6 24.4 %reduce-scatter.9.cloned.1.call-done = bf16[96,768]{1,0:T(8,128)(2,1)} async-done(((bf16[768,768]{1,0:T(8,128)(2,1)}), bf16[96,768]{1,0:T(8,128)(2,1)}) %reduce-scatter.9.cloned.1.call-update) | async-done | bytes 147472 | tf_op jit(solution)/shard_map/reduce_scatter | solution.py:873
  381.1 1.1 reshape.162
  382.2 13.1 %all_gather.25 = bf16[96,8,4,96]{3,1,0,2:T(8,128)(2,1)S(1)} all-gather(bf16[96,8,1,96]{3,1,0,2:T(8,128)(2,1)S(1)} %reshape.162), channel_id=1, replica_groups=mesh['seq'=2,'ctx'=4,'fsdp'=4] {'ctx'}, dimensions={2}, use_global_device_ids=true | all-gather | bytes 737280 | tf_op jit(solution)/shard_map/all_gather | solution.py:873
  395.3 1.0 copy.83
  396.3 2.6 reshape.168
  399.0 20.2 %reduce-scatter.11.cloned.1.call-done = bf16[96,768]{1,0:T(8,128)(2,1)} async-done(((bf16[768,768]{1,0:T(8,128)(2,1)}), bf16[96,768]{1,0:T(8,128)(2,1)}) %reduce-scatter.11.cloned.1.call-update) | async-done | bytes 147472 | tf_op jit(solution)/shard_map/reduce_scatter | solution.py:872
  419.2 13.5 %all_gather.27 = bf16[384,768]{1,0:T(8,128)(2,1)S(1)} all-gather(bf16[96,768]{1,0:T(8,128)(2,1)} %reduce-scatter.11.cloned.1.call-done), channel_id=1, replica_groups=mesh['seq'=2,'ctx'=4,'fsdp'=4] {'ctx'}, dimensions={0}, use_global_device_ids=true | all-gather | bytes 737280 | tf_op jit(solution)/shard_map/all_gather | solution.py:872
  432.7 1.1 convert_element_type.24
  433.7 37.4 %all-reduce.5.cloned.1.call-done = (bf16[96,2304]{0,1:T(8,128)(2,1)}, bf16[96,768]{1,0:T(8,128)(2,1)}) async-done(((bf16[96,2304]{0,1:T(8,128)(2,1)}, bf16[96,768]{1,0:T(8,128)(2,1)}), (bf16[96,2304]{0,1:T(8,128)(2,1)}, bf16[96,768]{1,0:T(8,128)(2,1)})) %all-reduce.5.cloned.1.call-update) | async-done | bytes 589840 | tf_op jit(solution)/shard_map/psum | solution.py:880
  471.2 2.2 copy.84
  (118 shorter events, 19.8 us)
Async XLA Ops:
  7.2 1.1 copy-start
  7.2 113.8 %all-gather.10.cloned.1.call-start = ((), (), s32[]{:S(2)}) async-start(), calls=%async_computation.6 | async-start | bytes 1327104 | tf_op jit(solution)/shard_map/all_gather | solution.py:862
  8.9 112.0 %all-gather.8.cloned.1.call-start = ((), (), s32[]{:S(2)}) async-start(), calls=%async_computation.5 | async-start | bytes 1327104 | tf_op jit(solution)/shard_map/all_gather | solution.py:861
  9.0 5.5 %copy-start.18 = (bf16[96]{0:T(256)(128)(2,1)S(1)}, bf16[96]{0:T(256)(128)(2,1)}, u32[]{:S(2)}) copy-start(bf16[96]{0:T(256)(128)(2,1)} %param.20) | copy-start | bytes 580
  9.0 5.6 %copy-start.19 = (bf16[96]{0:T(256)(128)(2,1)S(1)}, bf16[96]{0:T(256)(128)(2,1)}, u32[]{:S(2)}) copy-start(bf16[96]{0:T(256)(128)(2,1)} %param.19) | copy-start | bytes 580
  9.0 5.6 %copy-start.8 = (bf16[96,2304]{1,0:T(8,128)(2,1)S(1)}, bf16[96,2304]{1,0:T(8,128)(2,1)}, u32[]{:S(2)}) copy-start(bf16[96,2304]{1,0:T(8,128)(2,1)} %param.18) | copy-start | bytes 1327108
  13.5 107.5 %all-gather.6.cloned.1.call-start = ((), (), s32[]{:S(2)}) async-start(), calls=%async_computation.4 | async-start | bytes 1327104 | tf_op jit(solution)/shard_map/all_gather | solution.py:860
  14.2 290.9 %reduce-scatter.13.cloned.1.call-start = ((), (), s32[]{:S(2)}) async-start(), calls=%async_computation.10 | async-start | bytes 3981312
  15.7 0.9 copy-start.10
  15.7 0.9 copy-start.11
  15.7 0.9 copy-start.12
  16.0 23.8 %copy-start.16 = (s32[1,128]{1,0:T(1,128)S(1)}, s32[1,128]{1,0:T(1,128)}, u32[]{:S(2)}) copy-start(s32[1,128]{1,0:T(1,128)} %param.17) | copy-start | bytes 1540
  16.1 23.8 %copy-start.1 = (bf16[1,128,768]{2,1,0:T(8,128)(2,1)S(1)}, bf16[1,128,768]{2,1,0:T(8,128)(2,1)}, u32[]{:S(2)}) copy-start(bf16[1,128,768]{2,1,0:T(8,128)(2,1)} %param.16) | copy-start | bytes 589828
  39.9 81.1 %copy-start.2 = (bf16[1,128,768]{2,1,0:T(8,128)(2,1)S(1)}, bf16[1,128,768]{2,1,0:T(8,128)(2,1)}, u32[]{:S(2)}) copy-start(bf16[1,128,768]{2,1,0:T(8,128)(2,1)} %param.31) | copy-start | bytes 589828
  119.4 0.9 copy-start.3
  120.9 49.9 %copy-start.4 = (f32[512,128]{1,0:T(8,128)}, f32[512,128]{1,0:T(8,128)S(1)}, u32[]{:S(2)}) copy-start(f32[512,128]{1,0:T(8,128)S(1)} %get-tuple-element.38.lse_ref) | copy-start | bytes 786436
  121.0 49.9 %copy-start.7 = (s32[4,4,8,128]{3,2,1,0:T(8,128)S(1)}, s32[4,4,8,128]{3,2,1,0:T(8,128)}, u32[]{:S(2)}) copy-start(s32[4,4,8,128]{3,2,1,0:T(8,128)} %copy-done.6) | copy-start | bytes 196612
  170.9 1.0 copy-start.5
  227.0 116.2 %reduce-scatter.7.cloned.1.call-start = ((), (), s32[]{:S(2)}) async-start(), calls=%async_computation.7 | async-start | bytes 1327104 | tf_op jit(solution)/shard_map/reduce_scatter | solution.py:875
  227.6 153.5 %reduce-scatter.9.cloned.1.call-start = ((), (), s32[]{:S(2)}) async-start(), calls=%async_computation.8 | async-start | bytes 1327104 | tf_op jit(solution)/shard_map/reduce_scatter | solution.py:873
  227.6 1.3 copy-start.20
  228.1 191.0 %reduce-scatter.11.cloned.1.call-start = ((), (), s32[]{:S(2)}) async-start(), calls=%async_computation.9 | async-start | bytes 1327104 | tf_op jit(solution)/shard_map/reduce_scatter | solution.py:872
  228.9 242.3 %all-reduce.5.cloned.1.call-start = ((), (), s32[]{:S(2)}) async-start(), calls=%async_computation.11 | async-start | bytes 1474560 | tf_op jit(solution)/shard_map/psum | solution.py:880
  471.2 2.2 copy-start.9
  (5 other events, 4.1 us)
Sparse Core Ops, SparseCore 0:
  10.2 25.4 all-gather.9
  37.8 41.4 all-gather.7
  80.9 21.6 all-gather.5
  227.1 78.0 reduce-scatter.12
  307.4 35.8 reduce-scatter.6
  345.5 35.5 reduce-scatter.8
  383.4 35.6 reduce-scatter.10
  423.2 47.9 all-reduce.4
